TPU v7x, 32 devices: a whole 2x2x4 slice. The times are simulated.
32 devices in a mesh: shard: 4 (over y, x), ctx: 4 (over z), tp: 2 (over core).
Axes of the slice: x: 2, y: 2, z: 4, core: 2. Of those that a mesh axis runs over, the one named last changes fastest.
Arguments:
- inputs: bfloat16 [4096, 1024], P(('shard', 'ctx')), may hold values from -6 to 6
- lengths: int32 [4, 3], P('shard'), may hold values from 1 to 768, 1024 in all within a row
- cotangent: bfloat16 [4096, 1024], P(('shard', 'ctx')), may hold values from -6 to 6
- w_qkv: bfloat16 [3, 1024, 1024], P(None, 'shard', 'tp'), may hold values from -0.1875 to 0.1875
- w_out: bfloat16 [1024, 1024], P('tp', 'shard'), may hold values from -0.5 to 0.5
- w_fc: bfloat16 [1024, 4096], P('shard', 'tp'), may hold values from -0.1875 to 0.1875
- w_proj: bfloat16 [4096, 1024], P('tp', 'shard'), may hold values from -0.09375 to 0.09375
- b_qv: float32 [2, 1024], P(None, 'tp'), may hold values from -3 to 3
- b_out: float32 [1024], replicated, may hold values from -2 to 2
- b_fc: float32 [4096], P('tp'), may hold values from -3 to 3
- b_proj: float32 [1024], replicated, may hold values from -2 to 2
- ln1_gain: float32 [1024], replicated, may hold values from 0.25 to 1.75
- ln1_bias: float32 [1024], replicated, may hold values from -2 to 2
- ln2_gain: float32 [1024], replicated, may hold values from 0.25 to 1.75
- ln2_bias: float32 [1024], replicated, may hold values from -2 to 2
Outputs:
- outputs: bfloat16 [4096, 1024], P(('shard', 'ctx'))
- grad_inputs: bfloat16 [4096, 1024], P(('shard', 'ctx'))
- grad_w_qkv: float32 [3, 1024, 1024], P(None, 'shard', 'tp')
- grad_w_out: float32 [1024, 1024], P('tp', 'shard')
- grad_w_fc: float32 [1024, 4096], P('shard', 'tp')
- grad_w_proj: float32 [4096, 1024], P('tp', 'shard')
- grad_b_qv: float32 [2, 1024], P(None, 'tp')
- grad_b_out: float32 [1024], replicated
- grad_b_fc: float32 [4096], P('tp')
- grad_b_proj: float32 [1024], replicated
- grad_ln1_gain: float32 [1024], replicated
- grad_ln1_bias: float32 [1024], replicated
- grad_ln2_gain: float32 [1024], replicated
- grad_ln2_bias: float32 [1024], replicated
Inputs may be any that keep to these rules, and one draw needn't show every extreme that they name: Each row holds the lengths of one shard's 3 sequences in order; they sum to 1024, and the largest is 768.
All inputs are finite; a program needn't handle non-finite values.
Results may differ from a plain program's by a relative error of at most 0.02.
Values may be sent and summed in bfloat16 or wider, within the bound.
A program may use at most 128 MiB of HBM per device.

v0:
```python
import jax
import jax.numpy as jnp
from jax import lax
from jax.sharding import PartitionSpec as P

HEAD_DIM = 64


def layer_norm(values, gain, shift):
    mean = jnp.mean(values, axis=-1, keepdims=True)
    centred = values - mean
    spread = jnp.mean(centred * centred, axis=-1, keepdims=True)
    return centred * lax.rsqrt(spread + 1e-05) * gain + shift


def gelu_tanh(values):
    return (
        0.5
        * values
        * (1.0 + jnp.tanh(0.7978845608028654 * (values + 0.044715 * values * values * values)))
    )


def segment_ids(lengths, count):
    ends = jnp.cumsum(lengths)
    places = jnp.arange(count, dtype=jnp.int32)
    return jnp.sum((places[:, None] >= ends[None, :]).astype(jnp.int32), axis=1)


def dot32(left, right):
    return jnp.dot(left, right, preferred_element_type=jnp.float32)


def on_device(
    inputs,
    lengths,
    cotangent,
    w_qkv,
    w_out,
    w_fc,
    w_proj,
    b_qv,
    b_out,
    b_fc,
    b_proj,
    ln1_gain,
    ln1_bias,
    ln2_gain,
    ln2_bias,
):
    bf = jnp.bfloat16
    f32 = jnp.float32
    rows = inputs.shape[0]
    parts = lax.axis_size("ctx")
    block = rows * parts
    local_width = b_qv.shape[1]
    local_heads = local_width // HEAD_DIM
    seg_all = segment_ids(lengths[0], block)
    first = lax.axis_index("ctx") * rows
    q_pos = first + jnp.arange(rows, dtype=jnp.int32)
    q_seg = lax.dynamic_slice_in_dim(seg_all, first, rows)
    wq_all, wo_all, wfc_all, wproj_all = (
        lax.all_gather(w_qkv, "shard", axis=1, tiled=True),
        lax.all_gather(w_out, "shard", axis=1, tiled=True),
        lax.all_gather(w_fc, "shard", axis=0, tiled=True),
        lax.all_gather(w_proj, "shard", axis=1, tiled=True),
    )
    x_f = inputs.astype(f32)
    normed1 = layer_norm(x_f, ln1_gain, ln1_bias).astype(bf)
    query = ((dot32(normed1, wq_all[0]) + b_qv[0]) * 0.125).astype(bf)
    key = dot32(normed1, wq_all[1]).astype(bf)
    value = (dot32(normed1, wq_all[2]) + b_qv[1]).astype(bf)
    q3 = query.reshape(rows, local_heads, HEAD_DIM)

    def allowed_for(start, count):
        k_pos = start + jnp.arange(count, dtype=jnp.int32)
        k_seg = lax.dynamic_slice_in_dim(seg_all, start, count)
        return (k_pos[None, :] <= q_pos[:, None]) & (k_seg[None, :] == q_seg[:, None])

    k_piece = lax.all_gather(key, "ctx", axis=0, tiled=True)
    v_piece = lax.all_gather(value, "ctx", axis=0, tiled=True)
    count = k_piece.shape[0]
    allowed = allowed_for(jnp.int32(0), count)
    scores = jnp.einsum(
        "rhd,nhd->hrn",
        q3,
        k_piece.reshape(count, local_heads, HEAD_DIM),
        preferred_element_type=f32,
    )
    weights = jnp.where(allowed[None], jnp.exp(scores), 0.0)
    total = jnp.sum(weights, axis=2)
    acc = jnp.einsum(
        "hrn,nhd->hrd",
        weights.astype(bf),
        v_piece.reshape(count, local_heads, HEAD_DIM),
        preferred_element_type=f32,
    )
    total, acc = (total, acc)
    log_total = jnp.log(total)
    attended = (acc / total[:, :, None]).transpose(1, 0, 2).reshape(rows, local_width).astype(bf)
    mixed = lax.psum(dot32(attended, wo_all).astype(jnp.bfloat16), "tp").astype(jnp.float32)
    hidden = x_f + mixed + b_out
    normed2 = layer_norm(hidden, ln2_gain, ln2_bias).astype(bf)
    pre = dot32(normed2, wfc_all) + b_fc
    act = gelu_tanh(pre).astype(bf)
    mlp_total = lax.psum(dot32(act, wproj_all).astype(jnp.bfloat16), "tp").astype(jnp.float32)
    outputs = (hidden + mlp_total + b_proj).astype(bf)
    wq_back, wo_back, wfc_back, wproj_back = (
        lax.all_gather(w_qkv, "shard", axis=1, tiled=True),
        lax.all_gather(w_out, "shard", axis=1, tiled=True),
        lax.all_gather(w_fc, "shard", axis=0, tiled=True),
        lax.all_gather(w_proj, "shard", axis=1, tiled=True),
    )
    grad_f = cotangent.astype(f32)
    g_bproj = jnp.sum(grad_f, axis=0)
    g_proj = dot32(act.T, cotangent)
    d_act = dot32(cotangent, wproj_back.T)
    gelu_back = jax.vjp(gelu_tanh, pre)[1]
    d_pre = gelu_back(d_act)[0]
    g_bfc = jnp.sum(d_pre, axis=0)
    d_pre_b = d_pre.astype(bf)
    g_fc = dot32(normed2.T, d_pre_b)
    d_normed2 = lax.psum(dot32(d_pre_b, wfc_back.T).astype(jnp.bfloat16), "tp").astype(jnp.float32)
    norm_back2 = jax.vjp(layer_norm, hidden, ln2_gain, ln2_bias)[1]
    d_norm2, g_ln2g, g_ln2b = norm_back2(d_normed2)
    d_hidden = grad_f + d_norm2
    g_bout = jnp.sum(d_hidden, axis=0)
    d_hidden_b = d_hidden.astype(bf)
    g_out = dot32(attended.T, d_hidden_b)
    d_attended = dot32(d_hidden_b, wo_back.T).astype(bf)
    da3 = d_attended.reshape(rows, local_heads, HEAD_DIM)
    at3 = attended.reshape(rows, local_heads, HEAD_DIM)
    delta = jnp.einsum("rhd,rhd->hr", da3, at3, preferred_element_type=f32)
    key_all, value_all = (
        lax.all_gather(key, "ctx", axis=0, tiled=True),
        lax.all_gather(value, "ctx", axis=0, tiled=True),
    )
    key_blocks = key_all.reshape(parts, rows, local_heads, HEAD_DIM)
    value_blocks = value_all.reshape(parts, rows, local_heads, HEAD_DIM)
    starts = jnp.arange(parts, dtype=jnp.int32) * rows

    def back_piece(d_query_acc, inputs_piece):
        k_piece, v_piece, start = inputs_piece
        allowed = allowed_for(start, rows)
        scores = jnp.einsum("rhd,nhd->hrn", q3, k_piece, preferred_element_type=f32)
        probs = jnp.where(allowed[None], jnp.exp(scores - log_total[:, :, None]), 0.0)
        d_v = jnp.einsum("hrn,rhd->nhd", probs.astype(bf), da3, preferred_element_type=f32)
        d_probs = jnp.einsum("rhd,nhd->hrn", da3, v_piece, preferred_element_type=f32)
        d_scores_b = (probs * (d_probs - delta[:, :, None])).astype(bf)
        d_query_acc = d_query_acc + jnp.einsum(
            "hrn,nhd->rhd", d_scores_b, k_piece, preferred_element_type=f32
        )
        d_k = jnp.einsum("hrn,rhd->nhd", d_scores_b, q3, preferred_element_type=f32)
        return (d_query_acc, (d_k.reshape(rows, local_width), d_v.reshape(rows, local_width)))

    zero_query = jnp.zeros((rows, local_heads, HEAD_DIM), f32)
    d_query_acc, (d_key_terms, d_value_terms) = lax.scan(
        back_piece, zero_query, (key_blocks, value_blocks, starts)
    )
    d_key, d_value = (
        lax.psum_scatter(
            d_key_terms.reshape(block, local_width).astype(jnp.bfloat16),
            "ctx",
            scatter_dimension=0,
            tiled=True,
        ).astype(jnp.float32),
        lax.psum_scatter(
            d_value_terms.reshape(block, local_width).astype(jnp.bfloat16),
            "ctx",
            scatter_dimension=0,
            tiled=True,
        ).astype(jnp.float32),
    )
    d_query = d_query_acc.reshape(rows, local_width) * 0.125
    g_bqv = jnp.stack([jnp.sum(d_query, axis=0), jnp.sum(d_value, axis=0)])
    d_query_b = d_query.astype(bf)
    d_key_b = d_key.astype(bf)
    d_value_b = d_value.astype(bf)
    g_qkv = jnp.stack(
        [dot32(normed1.T, d_query_b), dot32(normed1.T, d_key_b), dot32(normed1.T, d_value_b)]
    )
    d_local = (
        dot32(d_query_b, wq_back[0].T)
        + dot32(d_key_b, wq_back[1].T)
        + dot32(d_value_b, wq_back[2].T)
    )
    d_normed1 = lax.psum(d_local.astype(jnp.bfloat16), "tp").astype(jnp.float32)
    norm_back1 = jax.vjp(layer_norm, x_f, ln1_gain, ln1_bias)[1]
    d_norm1, g_ln1g, g_ln1b = norm_back1(d_normed1)
    grad_inputs = (d_hidden + d_norm1).astype(bf)
    part_qkv, part_out, part_fc, part_proj = (
        lax.psum_scatter(
            g_qkv.astype(jnp.bfloat16), "shard", scatter_dimension=1, tiled=True
        ).astype(jnp.float32),
        lax.psum_scatter(
            g_out.astype(jnp.bfloat16), "shard", scatter_dimension=1, tiled=True
        ).astype(jnp.float32),
        lax.psum_scatter(
            g_fc.astype(jnp.bfloat16), "shard", scatter_dimension=0, tiled=True
        ).astype(jnp.float32),
        lax.psum_scatter(
            g_proj.astype(jnp.bfloat16), "shard", scatter_dimension=1, tiled=True
        ).astype(jnp.float32),
    )
    sum_qkv, sum_out, sum_fc, sum_proj = (
        lax.psum(part_qkv.astype(jnp.bfloat16), "ctx").astype(jnp.float32),
        lax.psum(part_out.astype(jnp.bfloat16), "ctx").astype(jnp.float32),
        lax.psum(part_fc.astype(jnp.bfloat16), "ctx").astype(jnp.float32),
        lax.psum(part_proj.astype(jnp.bfloat16), "ctx").astype(jnp.float32),
    )
    small = lax.psum(
        (g_bqv, g_bout, g_bfc, g_bproj, g_ln1g, g_ln1b, g_ln2g, g_ln2b), ("shard", "ctx")
    )
    return (
        outputs,
        grad_inputs,
        sum_qkv,
        sum_out,
        sum_fc,
        sum_proj,
        small[0],
        small[1],
        small[2],
        small[3],
        small[4],
        small[5],
        small[6],
        small[7],
    )


def solution(mesh):
    in_specs = (
        P(("shard", "ctx"), None),
        P("shard", None),
        P(("shard", "ctx"), None),
        P(None, "shard", "tp"),
        P("tp", "shard"),
        P("shard", "tp"),
        P("tp", "shard"),
        P(None, "tp"),
        P(),
        P("tp"),
        P(),
        P(),
        P(),
        P(),
        P(),
    )
    out_specs = (
        P(("shard", "ctx"), None),
        P(("shard", "ctx"), None),
        P(None, "shard", "tp"),
        P("tp", "shard"),
        P("shard", "tp"),
        P("tp", "shard"),
        P(None, "tp"),
        P(),
        P("tp"),
        P(),
        P(),
        P(),
        P(),
        P(),
    )
    return jax.shard_map(
        on_device, mesh=mesh, in_specs=in_specs, out_specs=out_specs, check_vma=False
    )
```

profile of v0, /device:TPU:0, one launch (start us, length us, event | category | flops | bytes accessed | tf_op | source)
XLA Modules:
  0.0 772.6 jit_solution(15052894565088602509)
XLA Ops:
  11.4 45.1 %all-gather.7.cloned.1.call-done = bf16[3,1024,512]{2,1,0:T(8,128)(2,1)} async-done(((bf16[3,256,512]{2,1,0:T(8,128)(2,1)}), bf16[3,1024,512]{2,1,0:T(8,128)(2,1)}) %all-gather.7.cloned.1.call-update) | async-done | bytes 3145744 | tf_op jit(solution)/shard_map/all_gather | solution.py:63
  56.4 2.6 fusion.47
  59.2 2.4 convolution_convert_fusion.10
  64.8 22.4 %all-gather.11.cloned.1.call-done = bf16[1024,512]{1,0:T(8,128)(2,1)} async-done(((bf16[256,512]{1,0:T(8,128)(2,1)}), bf16[1024,512]{1,0:T(8,128)(2,1)}) %all-gather.11.cloned.1.call-update) | async-done | bytes 1048592 | tf_op jit(solution)/shard_map/all_gather | solution.py:81
  88.7 28.1 %all-gather.9.cloned.1.call-done = bf16[1024,512]{1,0:T(8,128)(2,1)} async-done(((bf16[256,512]{1,0:T(8,128)(2,1)}), bf16[1024,512]{1,0:T(8,128)(2,1)}) %all-gather.9.cloned.1.call-update) | async-done | bytes 1048592 | tf_op jit(solution)/shard_map/all_gather | solution.py:80
  121.7 22.5 %all-gather.13.cloned.1.call-done = bf16[512,1024]{1,0:T(8,128)(2,1)} async-done(((bf16[512,256]{1,0:T(8,128)(2,1)}), bf16[512,1024]{1,0:T(8,128)(2,1)}) %all-gather.13.cloned.1.call-update) | async-done | bytes 1048592 | tf_op jit(solution)/shard_map/all_gather | solution.py:64
  144.2 2.5 convolution_convert_fusion.6
  148.2 17.4 %all-reduce.8.cloned.1.call-done = bf16[256,1024]{1,0:T(8,128)(2,1)} async-done(((bf16[256,1024]{1,0:T(8,128)(2,1)}), bf16[256,1024]{1,0:T(8,128)(2,1)}) %all-reduce.8.cloned.1.call-update) | async-done | bytes 524304 | tf_op jit(solution)/shard_map/psum | solution.py:101
  168.4 52.8 %all-gather.15.cloned.1.call-done = bf16[1024,2048]{1,0:T(8,128)(2,1)} async-done(((bf16[256,2048]{1,0:T(8,128)(2,1)}), bf16[1024,2048]{1,0:T(8,128)(2,1)}) %all-gather.15.cloned.1.call-update) | async-done | bytes 4194320 | tf_op jit(solution)/shard_map/all_gather | solution.py:65
  221.1 4.9 convolution_add_fusion
  226.0 49.4 %all-gather.17.cloned.1.call-done = bf16[2048,1024]{1,0:T(8,128)(2,1)} async-done(((bf16[2048,256]{1,0:T(8,128)(2,1)}), bf16[2048,1024]{1,0:T(8,128)(2,1)}) %all-gather.17.cloned.1.call-update) | async-done | bytes 4194320 | tf_op jit(solution)/shard_map/all_gather | solution.py:66
  275.4 7.6 fusion.86
  286.4 2.8 reshape.278
  291.2 2.8 reshape.279
  295.9 9.0 %all-reduce.10.cloned.1.call-done = bf16[256,1024]{1,0:T(8,128)(2,1)} async-done(((bf16[256,1024]{1,0:T(8,128)(2,1)}), bf16[256,1024]{1,0:T(8,128)(2,1)}) %all-reduce.10.cloned.1.call-update) | async-done | bytes 524304 | tf_op jit(solution)/shard_map/psum | solution.py:123
  312.3 53.9 %while.15 = (s32[]{:T(128)}, f32[256,8,64]{0,2,1:T(8,128)}, bf16[4,256,512]{2,1,0:T(8,128)(2,1)}, bf16[4,256,512]{2,1,0:T(8,128)(2,1)}, bf16[4,256,8,64]{1,3,2,0...) while((s32[]{:T(128)}, f32[256,8,64]{0,2,1:T(8,128)}, ...), condition=%wide.region_13.14_spmd.clone, body=%wide.region_12.13_spmd.clone.sunk | while | flops 340197888 | bytes 15172017 | solution.py:157
  345.8 2.2 fusion.145
  359.3 2.2 fusion.145
  368.9 3.4 convolution_convert_fusion.1
  373.4 5.2 convolution_convert_fusion
  381.4 13.5 %reduce-scatter.9.cloned.1.call-done = bf16[256,512]{1,0:T(8,128)(2,1)} async-done(((bf16[1024,512]{1,0:T(8,128)(2,1)}), bf16[256,512]{1,0:T(8,128)(2,1)}) %reduce-scatter.9.cloned.1.call-update) | async-done | bytes 262160 | tf_op jit(solution)/shard_map/reduce_scatter | solution.py:167
  394.8 2.5 fusion.38
  397.4 26.0 %reduce-scatter.7.cloned.1.call-done = bf16[256,512]{1,0:T(8,128)(2,1)} async-done(((bf16[1024,512]{1,0:T(8,128)(2,1)}), bf16[256,512]{1,0:T(8,128)(2,1)}) %reduce-scatter.7.cloned.1.call-update) | async-done | bytes 262160 | tf_op jit(solution)/shard_map/reduce_scatter | solution.py:161
  427.2 5.2 convolution_convert_fusion.8
  435.7 17.1 %reduce-scatter.13.cloned.1.call-done = bf16[512,256]{1,0:T(8,128)(2,1)} async-done(((bf16[512,1024]{1,0:T(8,128)(2,1)}), bf16[512,256]{1,0:T(8,128)(2,1)}) %reduce-scatter.13.cloned.1.call-update) | async-done | bytes 262160 | tf_op jit(solution)/shard_map/reduce_scatter | solution.py:195
  452.8 55.4 %reduce-scatter.15.cloned.1.call-done = bf16[256,2048]{1,0:T(8,128)(2,1)} async-done(((bf16[1024,2048]{1,0:T(8,128)(2,1)}), bf16[256,2048]{1,0:T(8,128)(2,1)}) %reduce-scatter.15.cloned.1.call-update) | async-done | bytes 1048592 | tf_op jit(solution)/shard_map/reduce_scatter | solution.py:198
  508.2 55.6 %reduce-scatter.17.cloned.1.call-done = bf16[2048,256]{1,0:T(8,128)(2,1)} async-done(((bf16[2048,1024]{1,0:T(8,128)(2,1)}), bf16[2048,256]{1,0:T(8,128)(2,1)}) %reduce-scatter.17.cloned.1.call-update) | async-done | bytes 1048592 | tf_op jit(solution)/shard_map/reduce_scatter | solution.py:201
  563.8 46.8 %reduce-scatter.11.cloned.1.call-done = bf16[3,256,512]{2,1,0:T(8,128)(2,1)} async-done(((bf16[3,1024,512]{2,1,0:T(8,128)(2,1)}), bf16[3,256,512]{2,1,0:T(8,128)(2,1)}) %reduce-scatter.11.cloned.1.call-update) | async-done | bytes 786448 | tf_op jit(solution)/shard_map/reduce_scatter | solution.py:192
  610.8 22.1 %all-reduce.14.cloned.1.call-done = (bf16[256,1024]{1,0:T(8,128)(2,1)}, bf16[256,1024]{1,0:T(8,128)(2,1)}) async-done(((bf16[256,1024]{1,0:T(8,128)(2,1)}, bf16[256,1024]{1,0:T(8,128)(2,1)}), (bf16[256,1024]{1,0:T(8,128)(2,1)}, bf16[256,1024]{1,0:T(8,128)(2,1)})) %all-reduce.14.cloned.1.call-update) | async-done | bytes 1048592 | tf_op jit(solution)/shard_map/psum | solution.py:106
  636.1 82.1 %all-reduce = (f32[2,512]{1,0:T(2,128)}, f32[1024]{0:T(1024)}, f32[2048]{0:T(1024)}, f32[1024]{0:T(1024)}, f32[1024]{0:T(1024)}, /*index=5*/f32[1024]{0:T(1024)}, f32[1024]{0:T(1024)}, f32[1024]{0:T(1024)}) all-reduce(f32[2,512]{1,0:T(2,128)S(1)} %pad_maximum_fusion.1, ...), channel_id=1, replica_groups=mesh['shard'=4,'ctx'=4,'tp'=2] {'shard','ctx'}, use_global_device_ids=true, to_apply=%region_29.30 | all-reduce | flops 9216 | bytes 73728 | tf_op jit(solution)/shard_map/psum | solution.py:211
  719.7 39.9 %all-reduce.12.cloned.1.call-done = (bf16[3,256,512]{2,1,0:T(8,128)(2,1)}, bf16[512,256]{1,0:T(8,128)(2,1)}, bf16[256,2048]{1,0:T(8,128)(2,1)}, bf16[2048,256]{1,0:T(8,128)(2,1)}) async-done(((bf16[3,256,512]{2,1,0:T(8,128)(2,1)}, bf16[512,256]{1,0:T(8,128)(2,1)}, bf16[256,2048]{1,0:T(8,128)(2,1)}, bf16[2048,256]{1,0:T(8,128)(2,1)}), (bf16[3,256,512]{2,1,0:T(8,128)(2,1)}, bf16[512,256]{1,0:T(8,128)(2,1)}, ...) | async-done | bytes 3145744 | tf_op jit(solution)/shard_map/psum | solution.py:206
  759.6 2.6 convert_element_type.168
  (227 shorter events, 96.0 us)
Async XLA Ops:
  7.2 49.3 %all-gather.7.cloned.1.call-start = ((), (), s32[]{:S(2)}) async-start(), calls=%async_computation.6 | async-start | bytes 3932160 | tf_op jit(solution)/shard_map/all_gather | solution.py:63
  7.9 79.3 %all-gather.11.cloned.1.call-start = ((), (), s32[]{:S(2)}) async-start(), calls=%async_computation.8 | async-start | bytes 1310720 | tf_op jit(solution)/shard_map/all_gather | solution.py:81
  9.2 50.0 %copy-start = (bf16[256,1024]{1,0:T(8,128)(2,1)S(1)}, bf16[256,1024]{1,0:T(8,128)(2,1)}, u32[]{:S(2)}) copy-start(bf16[256,1024]{1,0:T(8,128)(2,1)} %param.17) | copy-start | bytes 1572868
  9.2 50.0 %copy-start.30 = (f32[1024]{0:T(1024)S(1)}, f32[1024]{0:T(1024)}, u32[]{:S(2)}) copy-start(f32[1024]{0:T(1024)} %param.28) | copy-start | bytes 12292
  9.2 50.0 %copy-start.35 = (f32[1024]{0:T(1024)S(1)}, f32[1024]{0:T(1024)}, u32[]{:S(2)}) copy-start(f32[1024]{0:T(1024)} %param.29) | copy-start | bytes 12292
  59.1 57.7 %all-gather.9.cloned.1.call-start = ((), (), s32[]{:S(2)}) async-start(), calls=%async_computation.7 | async-start | bytes 1310720 | tf_op jit(solution)/shard_map/all_gather | solution.py:80
  61.6 82.6 %all-gather.13.cloned.1.call-start = ((), (), s32[]{:S(2)}) async-start(), calls=%async_computation.9 | async-start | bytes 1310720 | tf_op jit(solution)/shard_map/all_gather | solution.py:64
  62.2 103.4 %all-reduce.8.cloned.1.call-start = ((), (), s32[]{:S(2)}) async-start(), calls=%async_computation.10 | async-start | bytes 1048576 | tf_op jit(solution)/shard_map/psum | solution.py:101
  121.7 26.4 %copy-start.11 = (bf16[256,8,64]{0,2,1:T(8,128)(2,1)}, bf16[256,8,64]{0,2,1:T(8,128)(2,1)S(1)}, u32[]{:S(2)}) copy-start(bf16[256,8,64]{0,2,1:T(8,128)(2,1)S(1)} %fusion.62) | copy-start | bytes 786436
  144.2 21.4 %copy-start.25 = (f32[1024]{0:T(1024)S(1)}, f32[1024]{0:T(1024)}, u32[]{:S(2)}) copy-start(f32[1024]{0:T(1024)} %param.25) | copy-start | bytes 12292
  146.7 74.4 %copy-start.28 = (f32[1024]{0:T(1024)S(1)}, f32[1024]{0:T(1024)}, u32[]{:S(2)}) copy-start(f32[1024]{0:T(1024)} %param.30) | copy-start | bytes 12292
  146.8 74.4 %copy-start.29 = (f32[1024]{0:T(1024)S(1)}, f32[1024]{0:T(1024)}, u32[]{:S(2)}) copy-start(f32[1024]{0:T(1024)} %param.31) | copy-start | bytes 12292
  146.8 74.4 %copy-start.34 = (f32[2048]{0:T(1024)S(1)}, f32[2048]{0:T(1024)}, u32[]{:S(2)}) copy-start(f32[2048]{0:T(1024)} %param.26) | copy-start | bytes 24580
  146.8 74.3 %all-gather.15.cloned.1.call-start = ((), (), s32[]{:S(2)}) async-start(), calls=%async_computation.11 | async-start | bytes 5242880 | tf_op jit(solution)/shard_map/all_gather | solution.py:65
  147.4 128.1 %all-gather.17.cloned.1.call-start = ((), (), s32[]{:S(2)}) async-start(), calls=%async_computation.12 | async-start | bytes 5242880 | tf_op jit(solution)/shard_map/all_gather | solution.py:66
  148.1 156.8 %all-reduce.10.cloned.1.call-start = ((), (), s32[]{:S(2)}) async-start(), calls=%async_computation.13 | async-start | bytes 1048576 | tf_op jit(solution)/shard_map/psum | solution.py:123
  165.6 55.5 %copy-start.2 = (bf16[256,1024]{1,0:T(8,128)(2,1)S(1)}, bf16[256,1024]{1,0:T(8,128)(2,1)}, u32[]{:S(2)}) copy-start(bf16[256,1024]{1,0:T(8,128)(2,1)} %all-reduce.8.cloned.1.call-done) | copy-start | bytes 1572868
  168.4 107.1 %copy-start.21 = (bf16[256,1024]{1,0:T(8,128)(2,1)S(1)}, bf16[256,1024]{1,0:T(8,128)(2,1)}, u32[]{:S(2)}) copy-start(bf16[256,1024]{1,0:T(8,128)(2,1)} %param.19) | copy-start | bytes 1572868
  275.4 8.6 %copy-start.33 = (bf16[1024,2048]{1,0:T(8,128)(2,1)S(1)}, bf16[1024,2048]{1,0:T(8,128)(2,1)}, u32[]{:S(2)}) copy-start(bf16[1024,2048]{1,0:T(8,128)(2,1)} %all-gather.15.cloned.1.call-done) | copy-start | bytes 12582916
  286.2 108.7 %reduce-scatter.9.cloned.1.call-start = ((), (), s32[]{:S(2)}) async-start(), calls=%async_computation.15 | async-start | bytes 1310720 | tf_op jit(solution)/shard_map/reduce_scatter | solution.py:167
  295.9 12.4 %copy-start.22 = (bf16[256,1024]{1,0:T(8,128)(2,1)S(1)}, bf16[256,1024]{1,0:T(8,128)(2,1)}, u32[]{:S(2)}) copy-start(bf16[256,1024]{1,0:T(8,128)(2,1)} %param.19) | copy-start | bytes 1572868
  366.2 57.2 %reduce-scatter.7.cloned.1.call-start = ((), (), s32[]{:S(2)}) async-start(), calls=%async_computation.14 | async-start | bytes 1310720 | tf_op jit(solution)/shard_map/reduce_scatter | solution.py:161
  366.8 86.0 %reduce-scatter.13.cloned.1.call-start = ((), (), s32[]{:S(2)}) async-start(), calls=%async_computation.17 | async-start | bytes 1310720 | tf_op jit(solution)/shard_map/reduce_scatter | solution.py:195
  368.9 139.3 %reduce-scatter.15.cloned.1.call-start = ((), (), s32[]{:S(2)}) async-start(), calls=%async_computation.18 | async-start | bytes 5242880 | tf_op jit(solution)/shard_map/reduce_scatter | solution.py:198
  372.4 191.4 %reduce-scatter.17.cloned.1.call-start = ((), (), s32[]{:S(2)}) async-start(), calls=%async_computation.19 | async-start | bytes 5242880 | tf_op jit(solution)/shard_map/reduce_scatter | solution.py:201
  378.6 232.0 %reduce-scatter.11.cloned.1.call-start = ((), (), s32[]{:S(2)}) async-start(), calls=%async_computation.16 | async-start | bytes 3932160 | tf_op jit(solution)/shard_map/reduce_scatter | solution.py:192
  427.2 205.8 %all-reduce.14.cloned.1.call-start = ((), (), s32[]{:S(2)}) async-start(), calls=%async_computation.21 | async-start | bytes 2097152 | tf_op jit(solution)/shard_map/psum | solution.py:106
  435.6 324.0 %all-reduce.12.cloned.1.call-start = ((), (), s32[]{:S(2)}) async-start(), calls=%async_computation.20 | async-start | bytes 6291456 | tf_op jit(solution)/shard_map/psum | solution.py:206
  610.6 25.5 %copy-start.31 = (f32[2048]{0:T(1024)S(1)}, f32[2048]{0:T(1024)}, u32[]{:S(2)}) copy-start(f32[2048]{0:T(1024)} %get-tuple-element.231) | copy-start | bytes 24580
  610.6 107.6 %copy-start.32 = (f32[1024]{0:T(1024)S(1)}, f32[1024]{0:T(1024)}, u32[]{:S(2)}) copy-start(f32[1024]{0:T(1024)} %param.27) | copy-start | bytes 12292
  632.9 85.3 %copy-start.8 = (bf16[256,1024]{1,0:T(8,128)(2,1)S(1)}, bf16[256,1024]{1,0:T(8,128)(2,1)}, u32[]{:S(2)}) copy-start(bf16[256,1024]{1,0:T(8,128)(2,1)} %get-tuple-element.230) | copy-start | bytes 1572868
  632.9 85.3 %copy-start.24 = (bf16[256,1024]{1,0:T(8,128)(2,1)S(1)}, bf16[256,1024]{1,0:T(8,128)(2,1)}, u32[]{:S(2)}) copy-start(bf16[256,1024]{1,0:T(8,128)(2,1)} %get-tuple-element.229) | copy-start | bytes 1572868
  (29 other events, 72.3 us)
Sparse Core Ops, SparseCore 0:
  9.8 46.5 all-gather.6
  59.2 27.9 all-gather.10
  89.4 27.3 all-gather.8
  118.4 25.7 all-gather.12
  147.0 18.5 all-reduce.7
  167.3 53.7 all-gather.14
  222.9 52.4 all-gather.16
  286.3 18.5 all-reduce.9
  366.3 28.4 reduce-scatter.8
  397.5 25.7 reduce-scatter.6
  426.3 26.4 reduce-scatter.12
  455.6 52.5 reduce-scatter.14
  511.2 52.5 reduce-scatter.16
  566.6 43.9 reduce-scatter.10
  613.4 19.4 all-reduce.13
  635.4 124.1 all-reduce.11
where the time goes:
time: 774 us; the launch traced here: 773 us
  waiting for transfers between devices  526 us (68%)
  matrix products  82.7 us (11%)
  blocking collectives  82.1 us (11%)
  local copies, waits for them, and re-layouts  30.8 us (4%)
  other arithmetic  27.4 us (4%)
  between operations  14.4 us (2%)
  loops' own time  8.03 us (1%)
    psum x1, blocking collectives, on_device(): lax.psum((g_bqv, g_bout, g_bfc, g_bproj, g_ln1g, g_ln1b, g_ln2g, g_ln2b),...  82.1 us
    reduce_scatter x1, waiting for transfers between devices, on_device(): lax.psum_scatter(g_proj.astype(jnp.bfloat16), 'shard', scatter_dimension=...  55.6 us
    reduce_scatter x1, waiting for transfers between devices, on_device(): lax.psum_scatter(g_fc.astype(jnp.bfloat16), 'shard', scatter_dimension=0,...  55.4 us
    all_gather x1, waiting for transfers between devices, on_device(): lax.all_gather(w_fc, 'shard', axis=0, tiled=True)  52.8 us
    all_gather x1, waiting for transfers between devices, on_device(): lax.all_gather(w_proj, 'shard', axis=1, tiled=True)  49.4 us
    dot_general x18, matrix products, dot32(): return jnp.dot(left, right, preferred_element_type=jnp.float32)  47.6 us
    reduce_scatter x1, waiting for transfers between devices, on_device(): lax.psum_scatter(g_qkv.astype(jnp.bfloat16), 'shard', scatter_dimension=1...  46.8 us
    all_gather x1, waiting for transfers between devices, on_device(): lax.all_gather(w_qkv, 'shard', axis=1, tiled=True)  45.1 us
  transfers between devices with their start and end apart: 16, of which 16 were waited for; matrix products, arithmetic and copies ran while one was open for 8% of the time, Pallas kernels for 0%

commit v1 on v0

--- a/solution.py
+++ b/solution.py
@@ -4,6 +4,18 @@
 from jax.sharding import PartitionSpec as P
 
 HEAD_DIM = 64
+
+
+def doubled_up(shard, axis, dim):
+    ways, here = (lax.axis_size(axis), lax.axis_index(axis))
+    grown, reach = (shard, 1)
+    while reach < ways:
+        theirs = lax.ppermute(grown, axis, [(d, d ^ reach) for d in range(ways)])
+        mine_first = jnp.concatenate([grown, theirs], axis=dim)
+        theirs_first = jnp.concatenate([theirs, grown], axis=dim)
+        grown = jnp.where(here & reach == 0, mine_first, theirs_first)
+        reach = 2 * reach
+    return grown
 
 
 def layer_norm(values, gain, shift):
@@ -62,7 +74,7 @@
     wq_all, wo_all, wfc_all, wproj_all = (
         lax.all_gather(w_qkv, "shard", axis=1, tiled=True),
         lax.all_gather(w_out, "shard", axis=1, tiled=True),
-        lax.all_gather(w_fc, "shard", axis=0, tiled=True),
+        doubled_up(w_fc, "shard", 0),
         lax.all_gather(w_proj, "shard", axis=1, tiled=True),
     )
     x_f = inputs.astype(f32)

time: 774 us -> 813 us (1.050)
  waiting for transfers between devices: 526 us -> 543 us
  matrix products: 82.7 us -> 90.9 us
    ppermute x0 -> x2, waiting for transfers between devices: none -> 99.4 us  [doubled_up(): theirs = lax.ppermute(grown, axis, [(d, d ^ reach) for d in range(ways)])]
    all_gather x1, waiting for transfers between devices: 49.4 us -> 0.01 us  [on_device(): lax.all_gather(w_proj, 'shard', axis=1, tiled=True)]
    psum x1, waiting for transfers between devices: 17.4 us -> 0.01 us  [on_device(): lax.psum(dot32(attended, wo_all).astype(jnp.bfloat16), 'tp')]
    all_gather x1, waiting for transfers between devices: 52.8 us -> 38.4 us  [on_device(): lax.all_gather(w_fc, 'shard', axis=0, tiled=True)]
    reduce_scatter x1, waiting for transfers between devices: 26 us -> 12.3 us  [on_device(): lax.psum_scatter(d_key_terms.reshape(block, local_width).astype(jnp.bfloa...]
    reduce_scatter x1, waiting for transfers between devices: 13.5 us -> 25.4 us  [on_device(): lax.psum_scatter(d_value_terms.reshape(block, local_width).astype(jnp.bfl...]
    dynamic_update_slice x12, local copies, waits for them, and re-layouts: 8.3 us -> 18.7 us  [on_device(): lax.scan(back_piece, zero_query, (key_blocks, value_blocks, starts))]
  transfers between devices with their start and end apart: 16 -> 18, of which waited for: 16 -> 16; matrix products, arithmetic and copies ran while one was open for 8% -> 9% of each run, Pallas kernels for 0% -> 0%
where the time goes in v1:
time: 813 us; the launch traced here: 811 us
  waiting for transfers between devices  543 us (67%)
  matrix products  90.9 us (11%)
  blocking collectives  82.1 us (10%)
  local copies, waits for them, and re-layouts  38.3 us (5%)
  other arithmetic  29.9 us (4%)
  between operations  14.4 us (2%)
    ppermute x2, waiting for transfers between devices, doubled_up(): theirs = lax.ppermute(grown, axis, [(d, d ^ reach) for d in range(ways)])  99.4 us
    psum x1, blocking collectives, on_device(): lax.psum((g_bqv, g_bout, g_bfc, g_bproj, g_ln1g, g_ln1b, g_ln2g, g_ln2b),...  82.1 us
    reduce_scatter x1, waiting for transfers between devices, on_device(): lax.psum_scatter(g_proj.astype(jnp.bfloat16), 'shard', scatter_dimension=...  55.6 us
    reduce_scatter x1, waiting for transfers between devices, on_device(): lax.psum_scatter(g_fc.astype(jnp.bfloat16), 'shard', scatter_dimension=0,...  55.5 us
    dot_general x18, matrix products, dot32(): return jnp.dot(left, right, preferred_element_type=jnp.float32)  53 us
    reduce_scatter x1, waiting for transfers between devices, on_device(): lax.psum_scatter(g_qkv.astype(jnp.bfloat16), 'shard', scatter_dimension=1...  46.8 us
    all_gather x1, waiting for transfers between devices, on_device(): lax.all_gather(w_qkv, 'shard', axis=1, tiled=True)  45.8 us
    psum x1, waiting for transfers between devices, on_device(): lax.psum(part_qkv.astype(jnp.bfloat16), 'ctx').astype(jnp.float32)  39.9 us
  transfers between devices with their start and end apart: 18, of which 16 were waited for; matrix products, arithmetic and copies ran while one was open for 9% of the time, Pallas kernels for 0%

profile of v1, /device:TPU:0, one launch (start us, length us, event | category | flops | bytes accessed | tf_op | source)
XLA Modules:
  0.0 811.2 jit_solution(7591847104517518965)
XLA Ops:
  10.6 45.8 %all-gather.7.cloned.1.call-done = bf16[3,1024,512]{2,1,0:T(8,128)(2,1)} async-done(((bf16[3,256,512]{2,1,0:T(8,128)(2,1)}), bf16[3,1024,512]{2,1,0:T(8,128)(2,1)}) %all-gather.7.cloned.1.call-update) | async-done | bytes 3145744 | tf_op jit(solution)/shard_map/all_gather | solution.py:75
  56.4 2.6 convolution_convert_fusion.10
  59.2 2.4 fusion.55
  64.8 22.4 %all-gather.9.cloned.1.call-done = bf16[1024,512]{1,0:T(8,128)(2,1)} async-done(((bf16[256,512]{1,0:T(8,128)(2,1)}), bf16[1024,512]{1,0:T(8,128)(2,1)}) %all-gather.9.cloned.1.call-update) | async-done | bytes 1048592 | tf_op jit(solution)/shard_map/all_gather | solution.py:92
  88.7 28.1 %all-gather.11.cloned.1.call-done = bf16[1024,512]{1,0:T(8,128)(2,1)} async-done(((bf16[256,512]{1,0:T(8,128)(2,1)}), bf16[1024,512]{1,0:T(8,128)(2,1)}) %all-gather.11.cloned.1.call-update) | async-done | bytes 1048592 | tf_op jit(solution)/shard_map/all_gather | solution.py:93
  121.7 22.5 %all-gather.13.cloned.1.call-done = bf16[512,1024]{1,0:T(8,128)(2,1)} async-done(((bf16[512,256]{1,0:T(8,128)(2,1)}), bf16[512,1024]{1,0:T(8,128)(2,1)}) %all-gather.13.cloned.1.call-update) | async-done | bytes 1048592 | tf_op jit(solution)/shard_map/all_gather | solution.py:76
  144.2 2.6 convolution_convert_fusion.6
  149.9 23.3 %collective-permute-done = bf16[256,2048]{1,0:T(8,128)(2,1)S(1)} collective-permute-done((bf16[256,2048]{1,0:T(8,128)(2,1)S(1)}, bf16[256,2048]{1,0:T(8,128)(2,1)S(1)}, u32[]{:S(2)}, u32[]{:S(2)}) %collective-permute-start) | collective-permute-done | bytes 1048608 | tf_op jit(solution)/shard_map/ppermute | solution.py:13
  173.2 2.3 maximum_select_fusion.4
  179.8 76.1 %collective-permute-done.1 = bf16[512,2048]{1,0:T(8,128)(2,1)} collective-permute-done((bf16[512,2048]{1,0:T(8,128)(2,1)}, bf16[512,2048]{1,0:T(8,128)(2,1)}, u32[]{:S(2)}, u32[]{:S(2)}) %collective-permute-start.1) | collective-permute-done | bytes 2097184 | tf_op jit(solution)/shard_map/ppermute | solution.py:13
  255.9 6.5 fusion.34
  262.4 8.0 fusion.95
  270.4 38.4 %all-gather.17.cloned.1.call-done = bf16[1024,2048]{1,0:T(8,128)(2,1)} async-done(((bf16[256,2048]{1,0:T(8,128)(2,1)}), bf16[1024,2048]{1,0:T(8,128)(2,1)}) %all-gather.17.cloned.1.call-update) | async-done | bytes 4194320 | tf_op jit(solution)/shard_map/all_gather | solution.py:123
  308.8 4.3 convolution_convert_fusion.7
  313.4 2.8 reshape.279
  318.2 2.8 reshape.278
  322.9 8.9 %all-reduce.10.cloned.1.call-done = bf16[256,1024]{1,0:T(8,128)(2,1)} async-done(((bf16[256,1024]{1,0:T(8,128)(2,1)}), bf16[256,1024]{1,0:T(8,128)(2,1)}) %all-reduce.10.cloned.1.call-update) | async-done | bytes 524304 | tf_op jit(solution)/shard_map/psum | solution.py:135
  338.3 67.0 %while.15 = (s32[]{:T(128)}, f32[256,8,64]{0,2,1:T(8,128)}, bf16[4,256,512]{2,1,0:T(8,128)(2,1)}, bf16[4,256,512]{2,1,0:T(8,128)(2,1)}, bf16[4,256,8,64]{1,3,2,0...) while((s32[]{:T(128)}, f32[256,8,64]{0,2,1:T(8,128)}, ...), condition=%wide.region_13.14_spmd.clone, body=%wide.region_12.13_spmd.clone.sunk | while | flops 340197888 | bytes 15174041 | solution.py:169
  408.0 4.6 convolution_convert_fusion.1
  413.7 5.2 convolution_convert_fusion
  421.7 12.3 %reduce-scatter.7.cloned.1.call-done = bf16[256,512]{1,0:T(8,128)(2,1)} async-done(((bf16[1024,512]{1,0:T(8,128)(2,1)}), bf16[256,512]{1,0:T(8,128)(2,1)}) %reduce-scatter.7.cloned.1.call-update) | async-done | bytes 262160 | tf_op jit(solution)/shard_map/reduce_scatter | solution.py:173
  434.0 2.5 fusion.45
  436.5 25.4 %reduce-scatter.9.cloned.1.call-done = bf16[256,512]{1,0:T(8,128)(2,1)} async-done(((bf16[1024,512]{1,0:T(8,128)(2,1)}), bf16[256,512]{1,0:T(8,128)(2,1)}) %reduce-scatter.9.cloned.1.call-update) | async-done | bytes 262160 | tf_op jit(solution)/shard_map/reduce_scatter | solution.py:179
  465.7 5.2 convolution_convert_fusion.8
  474.2 17.1 %reduce-scatter.13.cloned.1.call-done = bf16[512,256]{1,0:T(8,128)(2,1)} async-done(((bf16[512,1024]{1,0:T(8,128)(2,1)}), bf16[512,256]{1,0:T(8,128)(2,1)}) %reduce-scatter.13.cloned.1.call-update) | async-done | bytes 262160 | tf_op jit(solution)/shard_map/reduce_scatter | solution.py:207
  491.3 55.5 %reduce-scatter.15.cloned.1.call-done = bf16[256,2048]{1,0:T(8,128)(2,1)} async-done(((bf16[1024,2048]{1,0:T(8,128)(2,1)}), bf16[256,2048]{1,0:T(8,128)(2,1)}) %reduce-scatter.15.cloned.1.call-update) | async-done | bytes 1048592 | tf_op jit(solution)/shard_map/reduce_scatter | solution.py:210
  546.7 55.6 %reduce-scatter.17.cloned.1.call-done = bf16[2048,256]{1,0:T(8,128)(2,1)} async-done(((bf16[2048,1024]{1,0:T(8,128)(2,1)}), bf16[2048,256]{1,0:T(8,128)(2,1)}) %reduce-scatter.17.cloned.1.call-update) | async-done | bytes 1048592 | tf_op jit(solution)/shard_map/reduce_scatter | solution.py:213
  602.3 46.8 %reduce-scatter.11.cloned.1.call-done = bf16[3,256,512]{2,1,0:T(8,128)(2,1)} async-done(((bf16[3,1024,512]{2,1,0:T(8,128)(2,1)}), bf16[3,256,512]{2,1,0:T(8,128)(2,1)}) %reduce-scatter.11.cloned.1.call-update) | async-done | bytes 786448 | tf_op jit(solution)/shard_map/reduce_scatter | solution.py:204
  649.3 22.2 %all-reduce.14.cloned.1.call-done = (bf16[256,1024]{1,0:T(8,128)(2,1)}, bf16[256,1024]{1,0:T(8,128)(2,1)}) async-done(((bf16[256,1024]{1,0:T(8,128)(2,1)}, bf16[256,1024]{1,0:T(8,128)(2,1)}), (bf16[256,1024]{1,0:T(8,128)(2,1)}, bf16[256,1024]{1,0:T(8,128)(2,1)})) %all-reduce.14.cloned.1.call-update) | async-done | bytes 1048592 | tf_op jit(solution)/shard_map/psum | solution.py:118
  674.6 82.1 %all-reduce = (f32[2,512]{1,0:T(2,128)}, f32[1024]{0:T(1024)}, f32[2048]{0:T(1024)}, f32[1024]{0:T(1024)}, f32[1024]{0:T(1024)}, /*index=5*/f32[1024]{0:T(1024)}, f32[1024]{0:T(1024)}, f32[1024]{0:T(1024)}) all-reduce(f32[2,512]{1,0:T(2,128)S(1)} %pad_maximum_fusion.1, ...), channel_id=1, replica_groups=mesh['shard'=4,'ctx'=4,'tp'=2] {'shard','ctx'}, use_global_device_ids=true, to_apply=%region_29.30 | all-reduce | flops 9216 | bytes 73728 | tf_op jit(solution)/shard_map/psum | solution.py:223
  758.3 39.9 %all-reduce.12.cloned.1.call-done = (bf16[3,256,512]{2,1,0:T(8,128)(2,1)}, bf16[512,256]{1,0:T(8,128)(2,1)}, bf16[256,2048]{1,0:T(8,128)(2,1)}, bf16[2048,256]{1,0:T(8,128)(2,1)}) async-done(((bf16[3,256,512]{2,1,0:T(8,128)(2,1)}, bf16[512,256]{1,0:T(8,128)(2,1)}, bf16[256,2048]{1,0:T(8,128)(2,1)}, bf16[2048,256]{1,0:T(8,128)(2,1)}), (bf16[3,256,512]{2,1,0:T(8,128)(2,1)}, bf16[512,256]{1,0:T(8,128)(2,1)}, ...) | async-done | bytes 3145744 | tf_op jit(solution)/shard_map/psum | solution.py:218
  798.1 2.9 convert_element_type.172
  (232 shorter events, 111.8 us)
Async XLA Ops:
  7.2 49.3 %all-gather.7.cloned.1.call-start = ((), (), s32[]{:S(2)}) async-start(), calls=%async_computation.6 | async-start | bytes 3932160 | tf_op jit(solution)/shard_map/all_gather | solution.py:75
  7.9 79.3 %all-gather.9.cloned.1.call-start = ((), (), s32[]{:S(2)}) async-start(), calls=%async_computation.7 | async-start | bytes 1310720 | tf_op jit(solution)/shard_map/all_gather | solution.py:92
  9.2 50.0 %copy-start.32 = (f32[2,512]{1,0:T(2,128)S(1)}, f32[2,512]{1,0:T(2,128)}, u32[]{:S(2)}) copy-start(f32[2,512]{1,0:T(2,128)} %param.24) | copy-start | bytes 12292
  9.2 50.0 %copy-start = (bf16[256,1024]{1,0:T(8,128)(2,1)S(1)}, bf16[256,1024]{1,0:T(8,128)(2,1)}, u32[]{:S(2)}) copy-start(bf16[256,1024]{1,0:T(8,128)(2,1)} %param.17) | copy-start | bytes 1572868
  9.2 50.0 %copy-start.30 = (f32[1024]{0:T(1024)S(1)}, f32[1024]{0:T(1024)}, u32[]{:S(2)}) copy-start(f32[1024]{0:T(1024)} %param.28) | copy-start | bytes 12292
  9.2 50.0 %copy-start.35 = (f32[1024]{0:T(1024)S(1)}, f32[1024]{0:T(1024)}, u32[]{:S(2)}) copy-start(f32[1024]{0:T(1024)} %param.29) | copy-start | bytes 12292
  59.1 57.7 %all-gather.11.cloned.1.call-start = ((), (), s32[]{:S(2)}) async-start(), calls=%async_computation.8 | async-start | bytes 1310720 | tf_op jit(solution)/shard_map/all_gather | solution.py:93
  61.6 82.6 %all-gather.13.cloned.1.call-start = ((), (), s32[]{:S(2)}) async-start(), calls=%async_computation.9 | async-start | bytes 1310720 | tf_op jit(solution)/shard_map/all_gather | solution.py:76
  62.2 114.8 %all-reduce.8.cloned.1.call-start = ((), (), s32[]{:S(2)}) async-start(), calls=%async_computation.10 | async-start | bytes 1048576 | tf_op jit(solution)/shard_map/psum | solution.py:113
  146.8 115.6 %all-gather.15.cloned.1.call-start = ((), (), s32[]{:S(2)}) async-start(), calls=%async_computation.11 | async-start | bytes 5242880 | tf_op jit(solution)/shard_map/all_gather | solution.py:78
  147.4 161.4 %all-gather.17.cloned.1.call-start = ((), (), s32[]{:S(2)}) async-start(), calls=%async_computation.12 | async-start | bytes 5242880 | tf_op jit(solution)/shard_map/all_gather | solution.py:123
  148.2 183.7 %all-reduce.10.cloned.1.call-start = ((), (), s32[]{:S(2)}) async-start(), calls=%async_computation.13 | async-start | bytes 1048576 | tf_op jit(solution)/shard_map/psum | solution.py:135
  148.4 24.8 %collective-permute-start = (bf16[256,2048]{1,0:T(8,128)(2,1)S(1)}, bf16[256,2048]{1,0:T(8,128)(2,1)S(1)}, u32[]{:S(2)}, u32[]{:S(2)}) collective-permute-start(bf16[256,2048]{1,0:T(8,128)(2,1)S(1)} %copy-done.9), channel_id=1, source_target_pairs={{0,8},{8,0},{16,24},{24,16},{1,9},{9,1},{17,25},{25,17},{2,10},{10... | collective-permute-start | bytes 3145736 | tf_op jit(solution)/shard_map/ppermute | solution.py:13
  149.9 27.1 %copy-start.25 = (f32[1024]{0:T(1024)S(1)}, f32[1024]{0:T(1024)}, u32[]{:S(2)}) copy-start(f32[1024]{0:T(1024)} %param.25) | copy-start | bytes 12292
  175.5 80.4 %copy-start.28 = (f32[1024]{0:T(1024)S(1)}, f32[1024]{0:T(1024)}, u32[]{:S(2)}) copy-start(f32[1024]{0:T(1024)} %param.30) | copy-start | bytes 12292
  175.5 80.4 %copy-start.29 = (f32[1024]{0:T(1024)S(1)}, f32[1024]{0:T(1024)}, u32[]{:S(2)}) copy-start(f32[1024]{0:T(1024)} %param.31) | copy-start | bytes 12292
  175.5 80.4 %copy-start.34 = (f32[2048]{0:T(1024)S(1)}, f32[2048]{0:T(1024)}, u32[]{:S(2)}) copy-start(f32[2048]{0:T(1024)} %param.26) | copy-start | bytes 24580
  175.5 80.4 %collective-permute-start.1 = (bf16[512,2048]{1,0:T(8,128)(2,1)}, bf16[512,2048]{1,0:T(8,128)(2,1)}, u32[]{:S(2)}, u32[]{:S(2)}) collective-permute-start(bf16[512,2048]{1,0:T(8,128)(2,1)} %maximum_select_fusion.4), channel_id=1, source_target_pairs={{0,16},{8,24},{16,0},{24,8},{1,17},{9,25},{17,1},{25,9},{2,18},{10... | collective-permute-start | bytes 6291464 | tf_op jit(solution)/shard_map/ppermute | solution.py:13
  177.0 78.9 %copy-start.2 = (bf16[256,1024]{1,0:T(8,128)(2,1)S(1)}, bf16[256,1024]{1,0:T(8,128)(2,1)}, u32[]{:S(2)}) copy-start(bf16[256,1024]{1,0:T(8,128)(2,1)} %all-reduce.8.cloned.1.call-done) | copy-start | bytes 1572868
  179.8 82.7 %copy-start.21 = (bf16[256,1024]{1,0:T(8,128)(2,1)S(1)}, bf16[256,1024]{1,0:T(8,128)(2,1)}, u32[]{:S(2)}) copy-start(bf16[256,1024]{1,0:T(8,128)(2,1)} %param.19) | copy-start | bytes 1572868
  270.4 42.7 %copy-start.19 = (bf16[256,2048]{1,0:T(8,128)(2,1)}, bf16[256,2048]{1,0:T(8,128)(2,1)S(1)}, u32[]{:S(2)}) copy-start(bf16[256,2048]{1,0:T(8,128)(2,1)S(1)} %get-tuple-element.232) | copy-start | bytes 3145732
  313.1 120.9 %reduce-scatter.7.cloned.1.call-start = ((), (), s32[]{:S(2)}) async-start(), calls=%async_computation.14 | async-start | bytes 1310720 | tf_op jit(solution)/shard_map/reduce_scatter | solution.py:173
  405.3 56.6 %reduce-scatter.9.cloned.1.call-start = ((), (), s32[]{:S(2)}) async-start(), calls=%async_computation.15 | async-start | bytes 1310720 | tf_op jit(solution)/shard_map/reduce_scatter | solution.py:179
  405.9 85.4 %reduce-scatter.13.cloned.1.call-start = ((), (), s32[]{:S(2)}) async-start(), calls=%async_computation.17 | async-start | bytes 1310720 | tf_op jit(solution)/shard_map/reduce_scatter | solution.py:207
  408.0 138.7 %reduce-scatter.15.cloned.1.call-start = ((), (), s32[]{:S(2)}) async-start(), calls=%async_computation.18 | async-start | bytes 5242880 | tf_op jit(solution)/shard_map/reduce_scatter | solution.py:210
  412.7 189.6 %reduce-scatter.17.cloned.1.call-start = ((), (), s32[]{:S(2)}) async-start(), calls=%async_computation.19 | async-start | bytes 5242880 | tf_op jit(solution)/shard_map/reduce_scatter | solution.py:213
  418.9 230.2 %reduce-scatter.11.cloned.1.call-start = ((), (), s32[]{:S(2)}) async-start(), calls=%async_computation.16 | async-start | bytes 3932160 | tf_op jit(solution)/shard_map/reduce_scatter | solution.py:204
  465.7 205.8 %all-reduce.14.cloned.1.call-start = ((), (), s32[]{:S(2)}) async-start(), calls=%async_computation.21 | async-start | bytes 2097152 | tf_op jit(solution)/shard_map/psum | solution.py:118
  474.1 324.0 %all-reduce.12.cloned.1.call-start = ((), (), s32[]{:S(2)}) async-start(), calls=%async_computation.20 | async-start | bytes 6291456 | tf_op jit(solution)/shard_map/psum | solution.py:218
  649.1 107.6 %copy-start.33 = (f32[1024]{0:T(1024)S(1)}, f32[1024]{0:T(1024)}, u32[]{:S(2)}) copy-start(f32[1024]{0:T(1024)} %param.27) | copy-start | bytes 12292
  671.4 85.3 %copy-start.8 = (bf16[256,1024]{1,0:T(8,128)(2,1)S(1)}, bf16[256,1024]{1,0:T(8,128)(2,1)}, u32[]{:S(2)}) copy-start(bf16[256,1024]{1,0:T(8,128)(2,1)} %get-tuple-element.230) | copy-start | bytes 1572868
  671.5 85.3 %copy-start.24 = (bf16[256,1024]{1,0:T(8,128)(2,1)S(1)}, bf16[256,1024]{1,0:T(8,128)(2,1)}, u32[]{:S(2)}) copy-start(bf16[256,1024]{1,0:T(8,128)(2,1)} %get-tuple-element.229) | copy-start | bytes 1572868
  (31 other events, 142.4 us)
Sparse Core Ops, SparseCore 0:
  9.8 46.5 all-gather.6
  59.2 27.9 all-gather.8
  89.4 27.3 all-gather.10
  118.4 25.7 all-gather.12
  147.0 18.5 all-reduce.7
  167.3 87.0 all-gather.14
  256.2 52.5 all-gather.16
  313.2 18.5 all-reduce.9
  405.4 28.4 reduce-scatter.6
  436.1 25.7 reduce-scatter.8
  464.8 26.4 reduce-scatter.12
  494.1 52.5 reduce-scatter.14
  549.7 52.5 reduce-scatter.16
  605.2 43.8 reduce-scatter.10
  651.9 19.5 all-reduce.13
  673.9 124.1 all-reduce.11
